TPU v7x, 32 devices: a whole 2x2x4 slice. The times are simulated.
32 devices in a mesh: seq: 8 (over z, x), head: 4 (over y, core).
Axes of the slice: x: 2, y: 2, z: 4, core: 2. Of those that a mesh axis runs over, the one named last changes fastest.
Arguments:
- queries: bfloat16 [1024, 1536], P('seq', 'head'), may hold values from -8 to 8
- cell_types: int32 [1024], P('seq'), may hold values from 0 to 127
- promoters: int32 [1024], P('seq'), may hold values from 0 to 16383, as said below
- offsets: int32 [1024], P('seq'), may hold values from -64 to 64, as said below
- cell_embed: bfloat16 [128, 1536], P(None, 'head'), may hold values from -3 to 3
- bin_keys: bfloat16 [16384, 1536], P('seq', 'head'), may hold values from -6 to 6
- bin_values: bfloat16 [16384, 1536], P('seq', 'head'), may hold values from -6 to 6
- slopes: float32 [16], P('head'), may hold values from 1.280082e-05 to 0.05
- w_out: bfloat16 [1536, 1536], P('head'), may hold values from -0.15625 to 0.15625
Outputs:
- pooled_features: bfloat16 [1024, 1536], P('seq', 'head')
Inputs may be any that keep to these rules, and one draw needn't show every extreme that they name: `promoters`: the promoter of row r lies in bins (r // 128) * 2048 to (r // 128 + 1) * 2048 - 1; in each aligned block of 128 rows, the block's first row sits at the first of those bins and its second row at the last. `offsets`: in each aligned block of 128 rows the first row has offset -64 and the second row 64.
All inputs are finite; a program needn't handle non-finite values.
Results may differ from a plain program's by a relative error of at most 0.012.
Values may be sent and summed in bfloat16 or wider, within the bound.
A program may use at most 128 MiB of HBM per device.

v0:
```python
import functools

import jax
import jax.numpy as jnp
from jax import lax
from jax.experimental import pallas as pl
from jax.experimental.pallas import tpu as pltpu
from jax.sharding import PartitionSpec as P

HEAD_DIM = 96
RADIUS = 7812
SHIFT = 64
HOPS = 4
LANES = 128
CHUNK = 256
EXTRA = 16
LOG2E = 1.4426950408889634
FAR = -1e30


MESH = pl.DeviceIdType.MESH


def identity_mask(size):
    return lax.broadcasted_iota(jnp.int32, (size, size), 0) == lax.broadcasted_iota(
        jnp.int32, (size, size), 1
    )


def as_column(row):
    size = row.shape[1]
    return jnp.sum(jnp.where(identity_mask(size), row, 0.0), axis=1, keepdims=True)


def as_row(column):
    size = column.shape[0]
    return jnp.sum(jnp.where(identity_mask(size), column, 0.0), axis=0, keepdims=True)


def tiles_of(head):
    first = head * HEAD_DIM
    start = first // LANES * LANES
    stop = -(-(first + HEAD_DIM) // LANES) * LANES
    return first, start, stop


def attend(hop, signs, slots, pack_ref, k_ref, v_ref, slope_ref, score_ref, out_ref, stat_ref):
    bins = k_ref.shape[0]
    rows = pack_ref.shape[1] - EXTRA
    width = k_ref.shape[1]
    groups = width // HEAD_DIM
    count = len(signs)
    aheads = []
    for sign, slot in zip(signs, slots):
        corner = pack_ref[slot, rows:, :rows].astype(jnp.float32)
        within = as_column(corner[0:1] * 256.0 + corner[1:2])
        aheads.append(hop * bins - sign * within if hop >= 2 else sign * hop * bins - within)
    parts = [{} for _ in signs]
    for head in range(groups):
        first, start, stop = tiles_of(head)
        slope = slope_ref[head] * LOG2E
        lane = lax.broadcasted_iota(jnp.int32, (count * rows, stop - start), 1) + start
        query = [pack_ref[slot, :rows, start:stop] for slot in slots]
        query = jnp.concatenate(query, axis=0) if count > 1 else query[0]
        query = jnp.where((lane >= first) & (lane < first + HEAD_DIM), query, jnp.zeros_like(query))
        buffer = head % 2
        tops = [None] * count
        for begin in range(0, bins, CHUNK):
            raw = lax.dot_general(
                query,
                k_ref[begin : begin + CHUNK, start:stop],
                (((1,), (1,)), ((), ())),
                preferred_element_type=jnp.float32,
            )
            index = (lax.broadcasted_iota(jnp.int32, (1, CHUNK), 1) + begin).astype(jnp.float32)
            for i, sign in enumerate(signs):
                scaled = raw[i * rows : (i + 1) * rows] * (LOG2E * HEAD_DIM**-0.5)
                if hop < 2:
                    distance = jnp.abs(index + aheads[i])
                    score = scaled - slope * distance
                    if (hop + 1) * bins - 1 + SHIFT > RADIUS:
                        score = jnp.where(distance <= RADIUS, score, FAR)
                else:
                    signed = index * float(sign)
                    score = scaled - slope * signed
                    farthest = begin + CHUNK - 1 if sign > 0 else bins - 1 - begin
                    if hop * bins + farthest + SHIFT > RADIUS:
                        score = jnp.where(signed <= RADIUS - aheads[i], score, FAR)
                score_ref[buffer, i * rows : (i + 1) * rows, begin : begin + CHUNK] = score
                for lanes in range(0, CHUNK, LANES):
                    piece = score[:, lanes : lanes + LANES]
                    tops[i] = piece if tops[i] is None else jnp.maximum(tops[i], piece)
        peaks = [
            jnp.maximum(jnp.max(top, axis=1, keepdims=True), 0.1 * FAR) for top in tops
        ]
        totals = [None] * count
        gained = None
        for begin in range(0, bins, CHUNK):
            weights = []
            for i in range(count):
                exps = jnp.exp2(
                    score_ref[buffer, i * rows : (i + 1) * rows, begin : begin + CHUNK] - peaks[i]
                )
                for lanes in range(0, CHUNK, LANES):
                    piece = exps[:, lanes : lanes + LANES]
                    totals[i] = piece if totals[i] is None else totals[i] + piece
                weights.append(exps.astype(jnp.bfloat16))
            term = jnp.dot(
                jnp.concatenate(weights, axis=0) if count > 1 else weights[0],
                v_ref[begin : begin + CHUNK, start:stop],
                preferred_element_type=jnp.float32,
            )
            gained = term if gained is None else gained + term
        for i, slot in enumerate(slots):
            peak = peaks[i] - slope * aheads[i] if hop >= 2 else peaks[i]
            stat_ref[slot, head : head + 1, :] = as_row(peak)
            stat_ref[slot, groups + head : groups + head + 1, :] = as_row(
                jnp.sum(totals[i], axis=1, keepdims=True)
            )
            for tile in range(start, stop, LANES):
                parts[i].setdefault(tile, []).append(
                    (first, gained[i * rows : (i + 1) * rows, tile - start : tile - start + LANES])
                )
    for i, slot in enumerate(slots):
        for tile, pieces in parts[i].items():
            lane = lax.broadcasted_iota(jnp.int32, (rows, LANES), 1) + tile
            value = pieces[0][1]
            for first, piece in pieces[1:]:
                value = jnp.where(lane >= first, piece, value)
            out_ref[slot, :, tile : tile + LANES] = value.astype(jnp.bfloat16)


def attend_kernel(
    hops, seq_count, head_count,
    query_ref, type_ref, promoter_ref, offset_ref, embed_ref, k_hbm, v_hbm, w_hbm, slope_ref,
    result_ref,
    k_ref, v_ref, w_ref, pack_ref, out_ref, stat_ref, back_ref, back_stat_ref,
    score_ref, sum_ref, part_ref, head_ref,
    load_sem, q_send, q_recv, o_send, o_recv, s_send, s_recv, h_send, h_recv,
):
    position = lax.axis_index("seq")
    mine = lax.axis_index("head")
    rows, width = out_ref.shape[1:]
    groups = width // HEAD_DIM
    piece = result_ref.shape[1]
    loads = [
        pltpu.make_async_copy(src, dst, load_sem.at[i])
        for i, (src, dst) in enumerate(((k_hbm, k_ref), (v_hbm, v_ref), (w_hbm, w_ref)))
    ]
    for load in loads:
        load.start()

    def inside(index):
        return (index >= 0) & (index < seq_count)

    barrier = pltpu.get_barrier_semaphore()
    offsets = [sign * hop for hop in range(1, hops + 1) for sign in (1, -1)]
    for d in offsets:

        @pl.when(inside(position + d))
        def _(d=d):
            pl.semaphore_signal(
                barrier, inc=1, device_id=(position + d, mine), device_id_type=MESH
            )

    for r in range(1, head_count):
        pl.semaphore_signal(
            barrier, inc=1, device_id=(position, lax.rem(mine + r, head_count)), device_id_type=MESH
        )

    bins = k_ref.shape[0]
    chosen = (
        lax.broadcasted_iota(jnp.int32, (embed_ref.shape[0], rows), 0) == type_ref[...]
    ).astype(jnp.float32)
    embedded = jnp.dot(
        chosen.T.astype(jnp.bfloat16), embed_ref[...], preferred_element_type=jnp.float32
    )
    home = pack_ref.at[hops]
    home[:rows, :] = (query_ref[...].astype(jnp.float32) + embedded).astype(jnp.bfloat16)
    within = promoter_ref[...] + offset_ref[...] - position * bins
    high = lax.shift_right_arithmetic(within, 8)
    digit = lax.broadcasted_iota(jnp.int32, (EXTRA, rows), 0)
    corner = jnp.where(digit == 0, high, within - 256 * high).astype(jnp.float32)
    home[rows:, :] = jnp.zeros((EXTRA, width), jnp.bfloat16)
    home[rows:, :rows] = corner.astype(jnp.bfloat16)

    around = jnp.minimum(position, hops) + jnp.minimum(seq_count - 1 - position, hops)
    pl.semaphore_wait(barrier, around + head_count - 1)

    side = 1 - 2 * lax.rem(position, 2)
    partner = position + side

    def query_copy(source, slot, target, send):
        return pltpu.make_async_remote_copy(
            src_ref=pack_ref.at[source], dst_ref=pack_ref.at[slot], send_sem=q_send.at[send],
            recv_sem=q_recv.at[slot], device_id=(target, mine), device_id_type=MESH,
        )

    sends = [
        (True, lambda: query_copy(hops, hops + side, partner, 0)),
        (inside(position + 2), lambda: query_copy(hops, hops + 2, position + 2, 1)),
        (inside(position - 2), lambda: query_copy(hops, hops - 2, position - 2, 2)),
    ]
    onward, final = [], []
    for s, send in ((1, 3), (-1, 5)):
        onward += [
            (
                inside(position - 2 * s) & inside(position + 2 * s),
                lambda s=s, send=send: query_copy(
                    hops + 2 * s, hops + 4 * s, position + 2 * s, send
                ),
            ),
            (
                inside(position - 2 * s),
                lambda s=s, send=send: query_copy(
                    hops + 2 * s, hops + 2 * s + side, partner, send + 1
                ),
            ),
        ]
        final.append(
            (
                inside(position - 4 * s) & (side == -s),
                lambda s=s: query_copy(hops + 4 * s, hops + 3 * s, partner, 7),
            )
        )

    def each(entries, act):
        for condition, make in entries:
            if condition is True:
                act(make())
            else:

                @pl.when(condition)
                def _(make=make):
                    act(make())

    def arrived(d):
        @pl.when(inside(position - d))
        def _():
            query_copy(hops, d + hops, partner, 0).wait_recv()

    def out_copy(slot, target):
        return pltpu.make_async_remote_copy(
            src_ref=out_ref.at[slot], dst_ref=back_ref.at[slot], send_sem=o_send.at[slot],
            recv_sem=o_recv.at[slot], device_id=(target, mine), device_id_type=MESH,
        )

    def stat_copy(slot, target):
        return pltpu.make_async_remote_copy(
            src_ref=stat_ref.at[slot], dst_ref=back_stat_ref.at[slot], send_sem=s_send.at[slot],
            recv_sem=s_recv.at[slot], device_id=(target, mine), device_id_type=MESH,
        )

    each(sends, lambda copy: copy.start())

    for d in offsets:

        @pl.when(jnp.logical_not(inside(position - d)))
        def _(d=d):
            pack_ref[d + hops] = jnp.zeros((rows + EXTRA, width), jnp.bfloat16)

    loads[0].wait()
    loads[1].wait()

    arrived(2)
    arrived(-2)
    each(onward, lambda copy: copy.start())
    for hop in (2, 1, 4, 3):
        pair = (hop, -hop)
        if hop == 1:
            arrived(4)
            arrived(-4)
            each(final, lambda copy: copy.start())
        if hop in (1, 3):
            for d in pair:
                arrived(d)

        @pl.when(inside(position - hop) | inside(position + hop))
        def _(hop=hop, pair=pair):
            attend(
                hop, (1, -1), [d + hops for d in pair], pack_ref, k_ref, v_ref, slope_ref,
                score_ref, out_ref, stat_ref,
            )

        for d in pair:

            @pl.when(inside(position - d))
            def _(d=d):
                stat_copy(d + hops, position - d).start()
                out_copy(d + hops, position - d).start()

    attend(
        0, (1,), [hops], pack_ref, k_ref, v_ref, slope_ref, score_ref, out_ref, stat_ref
    )

    back_stat_ref[hops] = stat_ref[hops]
    for d in offsets:
        slot = d + hops

        @pl.when(inside(position + d))
        def _(d=d, slot=slot):
            stat_copy(slot, position + d).wait_recv()

        @pl.when(jnp.logical_not(inside(position + d)))
        def _(slot=slot):
            back_stat_ref[slot, :groups, :] = jnp.full((groups, rows), FAR, jnp.float32)
            back_stat_ref[slot, groups:, :] = jnp.zeros((groups, rows), jnp.float32)

    slots = 2 * hops + 1
    peak = back_stat_ref[0, :groups, :]
    for slot in range(1, slots):
        peak = jnp.maximum(peak, back_stat_ref[slot, :groups, :])
    factors = [jnp.exp2(back_stat_ref[slot, :groups, :] - peak) for slot in range(slots)]
    total = factors[0] * back_stat_ref[0, groups:, :]
    for slot in range(1, slots):
        total = total + factors[slot] * back_stat_ref[slot, groups:, :]
    lane = lax.broadcasted_iota(jnp.int32, (rows, width), 1)

    def spread(factor):
        columns = factor.T
        wide = columns[:, 0:1]
        for head in range(1, groups):
            wide = jnp.where(lane >= head * HEAD_DIM, columns[:, head : head + 1], wide)
        return wide

    sum_ref[...] = out_ref[hops].astype(jnp.float32) * spread(factors[hops] / total)
    for d in offsets:
        slot = d + hops

        @pl.when(inside(position + d))
        def _(d=d, slot=slot):
            out_copy(slot, position + d).wait_recv()
            sum_ref[...] += back_ref[slot].astype(jnp.float32) * spread(factors[slot] / total)

    pooled = sum_ref[...].astype(jnp.bfloat16)
    loads[2].wait()

    def head_copy(r, target):
        return pltpu.make_async_remote_copy(
            src_ref=part_ref.at[r - 1], dst_ref=head_ref.at[r - 1], send_sem=h_send.at[r - 1],
            recv_sem=h_recv.at[r - 1], device_id=(position, target), device_id_type=MESH,
        )

    def share(target):
        columns = pl.ds(pl.multiple_of(target * piece, piece), piece)
        return jnp.dot(pooled, w_ref[:, columns], preferred_element_type=jnp.float32)

    for r in range(1, head_count):
        target = lax.rem(mine + r, head_count)
        part_ref[r - 1] = share(target).astype(jnp.bfloat16)
        head_copy(r, target).start()
    result = share(mine)
    for r in range(1, head_count):
        head_copy(r, lax.rem(mine + r, head_count)).wait_recv()
        result = result + head_ref[r - 1].astype(jnp.float32)
    result_ref[...] = result

    each(sends + onward + final, lambda copy: copy.wait_send())
    for r in range(1, head_count):
        head_copy(r, lax.rem(mine + r, head_count)).wait_send()
    for d in offsets:

        @pl.when(inside(position - d))
        def _(d=d):
            stat_copy(d + hops, position - d).wait_send()
            out_copy(d + hops, position - d).wait_send()


def local(queries, cell_types, promoters, offsets, cell_embed, bin_keys, bin_values, slopes, w_out):
    seq_count = lax.axis_size("seq")
    bins = bin_keys.shape[0]
    rows, width = queries.shape
    groups = slopes.shape[0]
    hops = min(HOPS, seq_count - 1)
    head_count = lax.axis_size("head")
    slots = 2 * hops + 1
    piece = w_out.shape[1] // head_count
    vmem = pl.BlockSpec(memory_space=pltpu.VMEM)
    anywhere = pl.BlockSpec(memory_space=pl.ANY)
    result = pl.pallas_call(
        functools.partial(attend_kernel, hops, seq_count, head_count),
        out_shape=jax.ShapeDtypeStruct((rows, piece), jnp.float32),
        in_specs=[vmem] * 5 + [anywhere] * 3 + [pl.BlockSpec(memory_space=pltpu.SMEM)],
        out_specs=vmem,
        scratch_shapes=[
            pltpu.VMEM((bins, width), jnp.bfloat16),
            pltpu.VMEM((bins, width), jnp.bfloat16),
            pltpu.VMEM(w_out.shape, jnp.bfloat16),
            pltpu.VMEM((slots, rows + EXTRA, width), jnp.bfloat16),
            pltpu.VMEM((slots, rows, width), jnp.bfloat16),
            pltpu.VMEM((slots, 2 * groups, rows), jnp.float32),
            pltpu.VMEM((slots, rows, width), jnp.bfloat16),
            pltpu.VMEM((slots, 2 * groups, rows), jnp.float32),
            pltpu.VMEM((2, 2 * rows, bins), jnp.float32),
            pltpu.VMEM((rows, width), jnp.float32),
            pltpu.VMEM((head_count - 1, rows, piece), jnp.bfloat16),
            pltpu.VMEM((head_count - 1, rows, piece), jnp.bfloat16),
            pltpu.SemaphoreType.DMA((3,)),
        ]
        + [pltpu.SemaphoreType.DMA((slots,))] * 6
        + [pltpu.SemaphoreType.DMA((head_count - 1,))] * 2,
        compiler_params=pltpu.CompilerParams(collective_id=0, has_side_effects=True),
    )(
        queries,
        cell_types[None],
        promoters[None],
        offsets[None],
        cell_embed,
        bin_keys,
        bin_values,
        w_out,
        slopes,
    )
    return result.astype(jnp.bfloat16)


def solution(mesh):
    return jax.shard_map(
        local,
        mesh=mesh,
        in_specs=(
            P("seq", "head"),
            P("seq"),
            P("seq"),
            P("seq"),
            P(None, "head"),
            P("seq", "head"),
            P("seq", "head"),
            P("head"),
            P("head", None),
        ),
        out_specs=P("seq", "head"),
        check_vma=False,
    )
```

profile of v0, /device:TPU:1, one launch (start us, length us, event | category | flops | bytes accessed | tf_op | source)
XLA Modules:
  0.0 40.0 jit_solution(9545918947443018157)
XLA Ops:
  0.0 38.4 %shard_map.91 = f32[128,384]{1,0:T(8,128)} custom-call(bf16[128,384]{1,0:T(8,128)(2,1)} %query_ref.1, s32[1,128]{1,0:T(1,128)} %bitcast.3, s32[1,128]{1,0:T(1,128)} %bitcast.4, s32[1,128]{1,0:T(1,128)} %bitcast.5, bf16[128,384]{1,0:T(8,128)(2,1)} %embed_ref.1, bf16[2048,384]{1,0:T(8,128)(2,1)} %k_hbm.1, bf16[2048,384]{1,0:T(8,128)(2,1)} %v_hbm.1, ...), custom_call_target="tpu_custom_call" | custom-call | tf_op jit(solution)/shard_map/pallas_call | solution.py:380
  38.4 1.6 %convert_element_type.3 = bf16[128,384]{1,0:T(8,128)(2,1)} convert(f32[128,384]{1,0:T(8,128)} %shard_map.91) | non-fusion elementwise | flops 49152 | bytes 294912 | tf_op jit(solution)/shard_map/convert_element_type | solution.py:414
where the time goes:
time: 40.1 us; the launch traced here: 40 us
  Pallas kernels  38.4 us (96%)
  other arithmetic  1.58 us (4%)
    pallas_call x1, Pallas kernels, local(): pl.pallas_call(functools.partial(attend_kernel, hops, seq_count, head_cou...  38.4 us
    convert_element_type x1, other arithmetic, local(): return result.astype(jnp.bfloat16)  1.58 us

commit v1 on v0

--- a/solution.py
+++ b/solution.py
@@ -21,126 +21,160 @@
 MESH = pl.DeviceIdType.MESH
 
 
-def identity_mask(size):
-    return lax.broadcasted_iota(jnp.int32, (size, size), 0) == lax.broadcasted_iota(
-        jnp.int32, (size, size), 1
-    )
-
-
-def as_column(row):
-    size = row.shape[1]
-    return jnp.sum(jnp.where(identity_mask(size), row, 0.0), axis=1, keepdims=True)
-
-
-def as_row(column):
-    size = column.shape[0]
-    return jnp.sum(jnp.where(identity_mask(size), column, 0.0), axis=0, keepdims=True)
-
-
-def tiles_of(head):
-    first = head * HEAD_DIM
-    start = first // LANES * LANES
-    stop = -(-(first + HEAD_DIM) // LANES) * LANES
-    return first, start, stop
-
-
-def attend(hop, signs, slots, pack_ref, k_ref, v_ref, slope_ref, score_ref, out_ref, stat_ref):
-    bins = k_ref.shape[0]
+def placed(head):
+    tile, offset = divmod(head * HEAD_DIM, LANES)
+    return tile, offset, (offset + HEAD_DIM) % LANES
+
+
+def spare_lanes(shape, free):
+    lane = lax.broadcasted_iota(jnp.int32, shape, len(shape) - 1) - free
+    return lane, (lane >= 0) & (lane < LANES - HEAD_DIM)
+
+
+def head_tile(rows_ref, head):
+    tile, offset, _ = placed(head)
+    own = rows_ref[:, tile * LANES : (tile + 1) * LANES]
+    if offset + HEAD_DIM > LANES:
+        other = rows_ref[:, (tile + 1) * LANES : (tile + 2) * LANES]
+        lane = lax.broadcasted_iota(jnp.int32, own.shape, 1)
+        own = jnp.where(lane >= offset, own, other)
+    return own
+
+
+def prepare_keys(k_ref, keys_ref):
+    for begin in range(0, k_ref.shape[0], CHUNK):
+        index = lax.broadcasted_iota(jnp.int32, (CHUNK, LANES), 0) + begin
+        for head in range(keys_ref.shape[0]):
+            _, _, free = placed(head)
+            lane, inner = spare_lanes((CHUNK, LANES), free)
+            part = jnp.where(lane % 2 == 0, index // 256, index % 256)
+            part = part.astype(jnp.float32).astype(jnp.bfloat16)
+            tile = head_tile(k_ref.at[begin : begin + CHUNK], head)
+            keys_ref[head, begin : begin + CHUNK, :] = jnp.where(inner, part, tile)
+
+
+def prepare_values(v_ref, values_ref):
+    for begin in range(0, v_ref.shape[0], CHUNK):
+        turned = v_ref[begin : begin + CHUNK, :].astype(jnp.float32).T.astype(jnp.bfloat16)
+        values_ref[:, begin : begin + CHUNK] = turned
+
+
+def prepare_query(rows_ref, head, slope, sign):
+    _, _, free = placed(head)
+    scaled = head_tile(rows_ref, head).astype(jnp.float32) * (LOG2E * HEAD_DIM**-0.5)
+    high = scaled.astype(jnp.bfloat16)
+    low = (scaled - high.astype(jnp.float32)).astype(jnp.bfloat16)
+    bias = jnp.full((1, LANES), slope * -sign, jnp.float32)
+    first = bias.astype(jnp.bfloat16).astype(jnp.float32)
+    second = (bias - first).astype(jnp.bfloat16).astype(jnp.float32)
+    third = (bias - first - second).astype(jnp.bfloat16).astype(jnp.float32)
+    lane, _ = spare_lanes((1, LANES), free)
+    weight = jnp.where(lane % 2 == 0, 256.0, 1.0)
+    near, far = (lane >= 0) & (lane < 2), (lane >= 2) & (lane < 4)
+    upper = jnp.where(near, first, jnp.where(far, second, 0.0)) * weight
+    lower = jnp.where(near, third, 0.0) * weight
+    _, inner = spare_lanes(scaled.shape, free)
+    high = jnp.where(inner, upper.astype(jnp.bfloat16), high)
+    low = jnp.where(inner, lower.astype(jnp.bfloat16), low)
+    return jnp.concatenate([high, low], axis=1)
+
+
+def attend(columns, slots, pack_ref, keys_ref, values_ref, slope_ref, score_ref, out_ref, stat_ref):
+    groups, bins, _ = keys_ref.shape
     rows = pack_ref.shape[1] - EXTRA
-    width = k_ref.shape[1]
-    groups = width // HEAD_DIM
-    count = len(signs)
-    aheads = []
-    for sign, slot in zip(signs, slots):
+    within = []
+    for slot in slots:
         corner = pack_ref[slot, rows:, :rows].astype(jnp.float32)
-        within = as_column(corner[0:1] * 256.0 + corner[1:2])
-        aheads.append(hop * bins - sign * within if hop >= 2 else sign * hop * bins - within)
-    parts = [{} for _ in signs]
-    for head in range(groups):
-        first, start, stop = tiles_of(head)
+        within.append(corner[0:1] * 256.0 + corner[1:2])
+    aheads = [hop * bins - sign * inside for (hop, sign), inside in zip(columns, within)]
+    first, last = bins, 0
+    for begin in range(0, bins, CHUNK):
+        for hop, sign in columns:
+            nearest = hop * bins + (begin - bins + 1 if sign > 0 else 1 - begin - CHUNK) - SHIFT
+            if hop < 2 or nearest <= RADIUS:
+                first, last = min(first, begin), max(last, begin + CHUNK)
+    sublane = lax.broadcasted_iota(jnp.int32, (8, rows), 0).astype(jnp.float32)
+
+    def biased(column, start, slope, score):
+        hop, sign = columns[column]
+        index = sublane + float(start)
+        if hop == 0 or (hop == 1 and (start < SHIFT if sign > 0 else start + 8 > bins - SHIFT)):
+            before = jnp.maximum(-(index * sign + aheads[column]), 0.0)
+            score = score - (2.0 * slope) * before
+        farthest = hop * bins + (start + 7 if sign > 0 else bins - 1 - start) + SHIFT
+        if farthest > RADIUS:
+            score = jnp.where(index * sign <= RADIUS - aheads[column], score, FAR)
+        return score
+
+    def scores(head):
         slope = slope_ref[head] * LOG2E
-        lane = lax.broadcasted_iota(jnp.int32, (count * rows, stop - start), 1) + start
-        query = [pack_ref[slot, :rows, start:stop] for slot in slots]
-        query = jnp.concatenate(query, axis=0) if count > 1 else query[0]
-        query = jnp.where((lane >= first) & (lane < first + HEAD_DIM), query, jnp.zeros_like(query))
-        buffer = head % 2
-        tops = [None] * count
-        for begin in range(0, bins, CHUNK):
+        query = [
+            prepare_query(pack_ref.at[slot, :rows], head, slope, float(sign))
+            for slot, (hop, sign) in zip(slots, columns)
+        ]
+        query = jnp.concatenate(query, axis=0) if len(slots) > 1 else query[0]
+        tops = [None] * len(slots)
+        for begin in range(first, last, CHUNK):
+            keys = keys_ref[head, begin : begin + CHUNK, :]
             raw = lax.dot_general(
+                jnp.concatenate([keys, keys], axis=1),
                 query,
-                k_ref[begin : begin + CHUNK, start:stop],
                 (((1,), (1,)), ((), ())),
                 preferred_element_type=jnp.float32,
             )
-            index = (lax.broadcasted_iota(jnp.int32, (1, CHUNK), 1) + begin).astype(jnp.float32)
-            for i, sign in enumerate(signs):
-                scaled = raw[i * rows : (i + 1) * rows] * (LOG2E * HEAD_DIM**-0.5)
-                if hop < 2:
-                    distance = jnp.abs(index + aheads[i])
-                    score = scaled - slope * distance
-                    if (hop + 1) * bins - 1 + SHIFT > RADIUS:
-                        score = jnp.where(distance <= RADIUS, score, FAR)
-                else:
-                    signed = index * float(sign)
-                    score = scaled - slope * signed
-                    farthest = begin + CHUNK - 1 if sign > 0 else bins - 1 - begin
-                    if hop * bins + farthest + SHIFT > RADIUS:
-                        score = jnp.where(signed <= RADIUS - aheads[i], score, FAR)
-                score_ref[buffer, i * rows : (i + 1) * rows, begin : begin + CHUNK] = score
-                for lanes in range(0, CHUNK, LANES):
-                    piece = score[:, lanes : lanes + LANES]
-                    tops[i] = piece if tops[i] is None else jnp.maximum(tops[i], piece)
-        peaks = [
-            jnp.maximum(jnp.max(top, axis=1, keepdims=True), 0.1 * FAR) for top in tops
-        ]
-        totals = [None] * count
-        gained = None
-        for begin in range(0, bins, CHUNK):
-            weights = []
-            for i in range(count):
-                exps = jnp.exp2(
-                    score_ref[buffer, i * rows : (i + 1) * rows, begin : begin + CHUNK] - peaks[i]
-                )
-                for lanes in range(0, CHUNK, LANES):
-                    piece = exps[:, lanes : lanes + LANES]
-                    totals[i] = piece if totals[i] is None else totals[i] + piece
-                weights.append(exps.astype(jnp.bfloat16))
-            term = jnp.dot(
-                jnp.concatenate(weights, axis=0) if count > 1 else weights[0],
-                v_ref[begin : begin + CHUNK, start:stop],
-                preferred_element_type=jnp.float32,
+            for start in range(0, CHUNK, 8):
+                for i in range(len(slots)):
+                    lanes = slice(i * rows, (i + 1) * rows)
+                    score = biased(i, begin + start, slope, raw[start : start + 8, lanes])
+                    score_ref[head % 2, begin + start : begin + start + 8, lanes] = score
+                    tops[i] = score if tops[i] is None else jnp.maximum(tops[i], score)
+        return [jnp.maximum(jnp.max(top, axis=0, keepdims=True), 0.1 * FAR) for top in tops]
+
+    def pool(head, peaks):
+        totals = [None] * len(slots)
+        weights = []
+        for begin in range(first, last, CHUNK):
+            parts = []
+            for i in range(len(slots)):
+                lanes = slice(i * rows, (i + 1) * rows)
+                exps = jnp.exp2(score_ref[head % 2, begin : begin + CHUNK, lanes] - peaks[i])
+                total = jnp.sum(exps.reshape(CHUNK // 8, 8, rows), axis=0)
+                totals[i] = total if totals[i] is None else totals[i] + total
+                parts.append(exps.astype(jnp.bfloat16))
+            weights.append(jnp.concatenate(parts, axis=1) if len(slots) > 1 else parts[0])
+        gained = jnp.dot(
+            values_ref[head * HEAD_DIM : (head + 1) * HEAD_DIM, first:last],
+            jnp.concatenate(weights, axis=0),
+            preferred_element_type=jnp.float32,
+        )
+        slope = slope_ref[head] * LOG2E
+        for i, slot in enumerate(slots):
+            out_ref[slot, head * HEAD_DIM : (head + 1) * HEAD_DIM, :] = gained[
+                :, i * rows : (i + 1) * rows
+            ].astype(jnp.bfloat16)
+            stat_ref[slot, head : head + 1, :] = peaks[i] - slope * aheads[i]
+            stat_ref[slot, groups + head : groups + head + 1, :] = jnp.sum(
+                totals[i], axis=0, keepdims=True
             )
-            gained = term if gained is None else gained + term
-        for i, slot in enumerate(slots):
-            peak = peaks[i] - slope * aheads[i] if hop >= 2 else peaks[i]
-            stat_ref[slot, head : head + 1, :] = as_row(peak)
-            stat_ref[slot, groups + head : groups + head + 1, :] = as_row(
-                jnp.sum(totals[i], axis=1, keepdims=True)
-            )
-            for tile in range(start, stop, LANES):
-                parts[i].setdefault(tile, []).append(
-                    (first, gained[i * rows : (i + 1) * rows, tile - start : tile - start + LANES])
-                )
-    for i, slot in enumerate(slots):
-        for tile, pieces in parts[i].items():
-            lane = lax.broadcasted_iota(jnp.int32, (rows, LANES), 1) + tile
-            value = pieces[0][1]
-            for first, piece in pieces[1:]:
-                value = jnp.where(lane >= first, piece, value)
-            out_ref[slot, :, tile : tile + LANES] = value.astype(jnp.bfloat16)
+
+    peaks = scores(0)
+    for head in range(groups):
+        later = scores(head + 1) if head + 1 < groups else None
+        pool(head, peaks)
+        peaks = later
 
 
 def attend_kernel(
     hops, seq_count, head_count,
     query_ref, type_ref, promoter_ref, offset_ref, embed_ref, k_hbm, v_hbm, w_hbm, slope_ref,
     result_ref,
-    k_ref, v_ref, w_ref, pack_ref, out_ref, stat_ref, back_ref, back_stat_ref,
+    k_ref, v_ref, keys_ref, values_ref, w_ref, pack_ref, out_ref, stat_ref, back_ref, back_stat_ref,
     score_ref, sum_ref, part_ref, head_ref,
     load_sem, q_send, q_recv, o_send, o_recv, s_send, s_recv, h_send, h_recv,
 ):
     position = lax.axis_index("seq")
     mine = lax.axis_index("head")
-    rows, width = out_ref.shape[1:]
+    width, rows = out_ref.shape[1:]
     groups = width // HEAD_DIM
     piece = result_ref.shape[1]
     loads = [
@@ -259,39 +293,43 @@
         def _(d=d):
             pack_ref[d + hops] = jnp.zeros((rows + EXTRA, width), jnp.bfloat16)
 
+    def run(columns, slots):
+        attend(
+            columns, slots, pack_ref, keys_ref, values_ref, slope_ref, score_ref, out_ref, stat_ref
+        )
+
+    def give(d):
+        @pl.when(inside(position - d))
+        def _():
+            stat_copy(d + hops, position - d).start()
+            out_copy(d + hops, position - d).start()
+
     loads[0].wait()
+    prepare_keys(k_ref, keys_ref)
     loads[1].wait()
-
+    prepare_values(v_ref, values_ref)
+    run([(0, 1)], [hops])
     arrived(2)
     arrived(-2)
     each(onward, lambda copy: copy.start())
     for hop in (2, 1, 4, 3):
-        pair = (hop, -hop)
         if hop == 1:
             arrived(4)
             arrived(-4)
             each(final, lambda copy: copy.start())
         if hop in (1, 3):
-            for d in pair:
+            for d in (hop, -hop):
                 arrived(d)
-
-        @pl.when(inside(position - hop) | inside(position + hop))
-        def _(hop=hop, pair=pair):
-            attend(
-                hop, (1, -1), [d + hops for d in pair], pack_ref, k_ref, v_ref, slope_ref,
-                score_ref, out_ref, stat_ref,
-            )
-
-        for d in pair:
-
-            @pl.when(inside(position - d))
-            def _(d=d):
-                stat_copy(d + hops, position - d).start()
-                out_copy(d + hops, position - d).start()
-
-    attend(
-        0, (1,), [hops], pack_ref, k_ref, v_ref, slope_ref, score_ref, out_ref, stat_ref
-    )
+        if hop == 4:
+            for d in (hop, -hop):
+
+                @pl.when(inside(position - d))
+                def _(d=d):
+                    run([(abs(d), 1 if d > 0 else -1)], [d + hops])
+        else:
+            run([(hop, 1), (hop, -1)], [hop + hops, hops - hop])
+        for d in (hop, -hop):
+            give(d)
 
     back_stat_ref[hops] = stat_ref[hops]
     for d in offsets:
@@ -314,25 +352,25 @@
     total = factors[0] * back_stat_ref[0, groups:, :]
     for slot in range(1, slots):
         total = total + factors[slot] * back_stat_ref[slot, groups:, :]
-    lane = lax.broadcasted_iota(jnp.int32, (rows, width), 1)
-
-    def spread(factor):
-        columns = factor.T
-        wide = columns[:, 0:1]
-        for head in range(1, groups):
-            wide = jnp.where(lane >= head * HEAD_DIM, columns[:, head : head + 1], wide)
-        return wide
-
-    sum_ref[...] = out_ref[hops].astype(jnp.float32) * spread(factors[hops] / total)
+
+    def scaled(part, factor):
+        part = part.astype(jnp.float32)
+        pieces = [
+            part[head * HEAD_DIM : (head + 1) * HEAD_DIM] * factor[head : head + 1]
+            for head in range(groups)
+        ]
+        return jnp.concatenate(pieces, axis=0)
+
+    sum_ref[...] = scaled(out_ref[hops], factors[hops] / total)
     for d in offsets:
         slot = d + hops
 
         @pl.when(inside(position + d))
         def _(d=d, slot=slot):
             out_copy(slot, position + d).wait_recv()
-            sum_ref[...] += back_ref[slot].astype(jnp.float32) * spread(factors[slot] / total)
-
-    pooled = sum_ref[...].astype(jnp.bfloat16)
+            sum_ref[...] += scaled(back_ref[slot], factors[slot] / total)
+
+    pooled = sum_ref[...].T.astype(jnp.bfloat16)
     loads[2].wait()
 
     def head_copy(r, target):
@@ -385,14 +423,16 @@
         scratch_shapes=[
             pltpu.VMEM((bins, width), jnp.bfloat16),
             pltpu.VMEM((bins, width), jnp.bfloat16),
+            pltpu.VMEM((groups, bins, LANES), jnp.bfloat16),
+            pltpu.VMEM((width, bins), jnp.bfloat16),
             pltpu.VMEM(w_out.shape, jnp.bfloat16),
             pltpu.VMEM((slots, rows + EXTRA, width), jnp.bfloat16),
-            pltpu.VMEM((slots, rows, width), jnp.bfloat16),
+            pltpu.VMEM((slots, width, rows), jnp.bfloat16),
             pltpu.VMEM((slots, 2 * groups, rows), jnp.float32),
-            pltpu.VMEM((slots, rows, width), jnp.bfloat16),
+            pltpu.VMEM((slots, width, rows), jnp.bfloat16),
             pltpu.VMEM((slots, 2 * groups, rows), jnp.float32),
-            pltpu.VMEM((2, 2 * rows, bins), jnp.float32),
-            pltpu.VMEM((rows, width), jnp.float32),
+            pltpu.VMEM((2, bins, 2 * rows), jnp.float32),
+            pltpu.VMEM((width, rows), jnp.float32),
             pltpu.VMEM((head_count - 1, rows, piece), jnp.bfloat16),
             pltpu.VMEM((head_count - 1, rows, piece), jnp.bfloat16),
             pltpu.SemaphoreType.DMA((3,)),

time: 40.1 us -> 37.1 us (0.925)
  Pallas kernels: 38.4 us -> 35.3 us
    pallas_call x1, Pallas kernels: 38.4 us -> 35.3 us  [local(): pl.pallas_call(functools.partial(attend_kernel, hops, seq_count, head_cou...]
where the time goes in v1:
time: 37.1 us; the launch traced here: 36.9 us
  Pallas kernels  35.3 us (95%)
  other arithmetic  1.58 us (4%)
    pallas_call x1, Pallas kernels, local(): pl.pallas_call(functools.partial(attend_kernel, hops, seq_count, head_cou...  35.3 us
    convert_element_type x1, other arithmetic, local(): return result.astype(jnp.bfloat16)  1.58 us

profile of v1, /device:TPU:1, one launch (start us, length us, event | category | flops | bytes accessed | tf_op | source)
XLA Modules:
  0.0 36.9 jit_solution(9688738927134029056)
XLA Ops:
  0.0 35.3 %shard_map.91 = f32[128,384]{1,0:T(8,128)} custom-call(bf16[128,384]{1,0:T(8,128)(2,1)} %query_ref.1, s32[1,128]{1,0:T(1,128)} %bitcast.3, s32[1,128]{1,0:T(1,128)} %bitcast.4, s32[1,128]{1,0:T(1,128)} %bitcast.5, bf16[128,384]{1,0:T(8,128)(2,1)} %embed_ref.1, bf16[2048,384]{1,0:T(8,128)(2,1)} %k_hbm.1, bf16[2048,384]{1,0:T(8,128)(2,1)} %v_hbm.1, ...), custom_call_target="tpu_custom_call" | custom-call | tf_op jit(solution)/shard_map/pallas_call | solution.py:418
  35.3 1.6 %convert_element_type.3 = bf16[128,384]{1,0:T(8,128)(2,1)} convert(f32[128,384]{1,0:T(8,128)} %shard_map.91) | non-fusion elementwise | flops 49152 | bytes 294912 | tf_op jit(solution)/shard_map/convert_element_type | solution.py:454

commit v2 on v1

--- a/solution.py
+++ b/solution.py
@@ -16,6 +16,7 @@
 EXTRA = 16
 LOG2E = 1.4426950408889634
 FAR = -1e30
+PIECES = 2
 
 
 MESH = pl.DeviceIdType.MESH
@@ -31,11 +32,11 @@
     return lane, (lane >= 0) & (lane < LANES - HEAD_DIM)
 
 
-def head_tile(rows_ref, head):
+def head_tile(tile_at, head):
     tile, offset, _ = placed(head)
-    own = rows_ref[:, tile * LANES : (tile + 1) * LANES]
+    own = tile_at(tile)
     if offset + HEAD_DIM > LANES:
-        other = rows_ref[:, (tile + 1) * LANES : (tile + 2) * LANES]
+        other = tile_at(tile + 1)
         lane = lax.broadcasted_iota(jnp.int32, own.shape, 1)
         own = jnp.where(lane >= offset, own, other)
     return own
@@ -49,7 +50,9 @@
             lane, inner = spare_lanes((CHUNK, LANES), free)
             part = jnp.where(lane % 2 == 0, index // 256, index % 256)
             part = part.astype(jnp.float32).astype(jnp.bfloat16)
-            tile = head_tile(k_ref.at[begin : begin + CHUNK], head)
+            tile = head_tile(
+                lambda t: k_ref[begin : begin + CHUNK, t * LANES : (t + 1) * LANES], head
+            )
             keys_ref[head, begin : begin + CHUNK, :] = jnp.where(inner, part, tile)
 
 
@@ -59,9 +62,9 @@
         values_ref[:, begin : begin + CHUNK] = turned
 
 
-def prepare_query(rows_ref, head, slope, sign):
+def prepare_query(tile_at, head, slope, sign):
     _, _, free = placed(head)
-    scaled = head_tile(rows_ref, head).astype(jnp.float32) * (LOG2E * HEAD_DIM**-0.5)
+    scaled = head_tile(tile_at, head).astype(jnp.float32) * (LOG2E * HEAD_DIM**-0.5)
     high = scaled.astype(jnp.bfloat16)
     low = (scaled - high.astype(jnp.float32)).astype(jnp.bfloat16)
     bias = jnp.full((1, LANES), slope * -sign, jnp.float32)
@@ -79,12 +82,14 @@
     return jnp.concatenate([high, low], axis=1)
 
 
-def attend(columns, slots, pack_ref, keys_ref, values_ref, slope_ref, score_ref, out_ref, stat_ref):
+def attend(
+    columns, slots, after, pack_ref, keys_ref, values_ref, slope_ref, score_ref, out_ref, stat_ref
+):
     groups, bins, _ = keys_ref.shape
-    rows = pack_ref.shape[1] - EXTRA
+    rows = out_ref.shape[2]
     within = []
     for slot in slots:
-        corner = pack_ref[slot, rows:, :rows].astype(jnp.float32)
+        corner = pack_ref[slot, :EXTRA, :rows].astype(jnp.float32)
         within.append(corner[0:1] * 256.0 + corner[1:2])
     aheads = [hop * bins - sign * inside for (hop, sign), inside in zip(columns, within)]
     first, last = bins, 0
@@ -109,7 +114,10 @@
     def scores(head):
         slope = slope_ref[head] * LOG2E
         query = [
-            prepare_query(pack_ref.at[slot, :rows], head, slope, float(sign))
+            prepare_query(
+                lambda t: pack_ref[slot, EXTRA + t * rows : EXTRA + (t + 1) * rows, :],
+                head, slope, float(sign),
+            )
             for slot, (hop, sign) in zip(slots, columns)
         ]
         query = jnp.concatenate(query, axis=0) if len(slots) > 1 else query[0]
@@ -162,6 +170,7 @@
         later = scores(head + 1) if head + 1 < groups else None
         pool(head, peaks)
         peaks = later
+        after(head)
 
 
 def attend_kernel(
@@ -210,13 +219,16 @@
         chosen.T.astype(jnp.bfloat16), embed_ref[...], preferred_element_type=jnp.float32
     )
     home = pack_ref.at[hops]
-    home[:rows, :] = (query_ref[...].astype(jnp.float32) + embedded).astype(jnp.bfloat16)
+    query = (query_ref[...].astype(jnp.float32) + embedded).astype(jnp.bfloat16)
+    for tile in range(width // LANES):
+        home[EXTRA + tile * rows : EXTRA + (tile + 1) * rows, :] = query[
+            :, tile * LANES : (tile + 1) * LANES
+        ]
     within = promoter_ref[...] + offset_ref[...] - position * bins
     high = lax.shift_right_arithmetic(within, 8)
     digit = lax.broadcasted_iota(jnp.int32, (EXTRA, rows), 0)
     corner = jnp.where(digit == 0, high, within - 256 * high).astype(jnp.float32)
-    home[rows:, :] = jnp.zeros((EXTRA, width), jnp.bfloat16)
-    home[rows:, :rows] = corner.astype(jnp.bfloat16)
+    home[:EXTRA, :] = corner.astype(jnp.bfloat16)
 
     around = jnp.minimum(position, hops) + jnp.minimum(seq_count - 1 - position, hops)
     pl.semaphore_wait(barrier, around + head_count - 1)
@@ -224,58 +236,68 @@
     side = 1 - 2 * lax.rem(position, 2)
     partner = position + side
 
-    def query_copy(source, slot, target, send):
+    length = pack_ref.shape[1]
+    cuts = [0, EXTRA + (length - EXTRA) // 2, length]
+
+    def query_copy(source, slot, target, send, k):
+        part = slice(cuts[k], cuts[k + 1])
         return pltpu.make_async_remote_copy(
-            src_ref=pack_ref.at[source], dst_ref=pack_ref.at[slot], send_sem=q_send.at[send],
-            recv_sem=q_recv.at[slot], device_id=(target, mine), device_id_type=MESH,
+            src_ref=pack_ref.at[source, part], dst_ref=pack_ref.at[slot, part],
+            send_sem=q_send.at[send, k], recv_sem=q_recv.at[slot, k],
+            device_id=(target, mine), device_id_type=MESH,
         )
 
     sends = [
-        (True, lambda: query_copy(hops, hops + side, partner, 0)),
-        (inside(position + 2), lambda: query_copy(hops, hops + 2, position + 2, 1)),
-        (inside(position - 2), lambda: query_copy(hops, hops - 2, position - 2, 2)),
+        (True, lambda k: query_copy(hops, hops + side, partner, 0, k)),
+        (inside(position + 2), lambda k: query_copy(hops, hops + 2, position + 2, 1, k)),
+        (inside(position - 2), lambda k: query_copy(hops, hops - 2, position - 2, 2, k)),
     ]
-    onward, final = [], []
+    onward, across, final = [], [], []
     for s, send in ((1, 3), (-1, 5)):
-        onward += [
+        onward.append(
             (
                 inside(position - 2 * s) & inside(position + 2 * s),
-                lambda s=s, send=send: query_copy(
-                    hops + 2 * s, hops + 4 * s, position + 2 * s, send
+                lambda k, s=s, send=send: query_copy(
+                    hops + 2 * s, hops + 4 * s, position + 2 * s, send, k
                 ),
-            ),
+            )
+        )
+        across.append(
             (
-                inside(position - 2 * s),
-                lambda s=s, send=send: query_copy(
-                    hops + 2 * s, hops + 2 * s + side, partner, send + 1
+                inside(position + 2 * s),
+                lambda k, s=s, send=send: query_copy(
+                    hops - side, hops + 2 * s - side, position + 2 * s, send + 1, k
                 ),
-            ),
-        ]
+            )
+        )
         final.append(
             (
                 inside(position - 4 * s) & (side == -s),
-                lambda s=s: query_copy(hops + 4 * s, hops + 3 * s, partner, 7),
-            )
-        )
-
-    def each(entries, act):
+                lambda k, s=s: query_copy(hops + 4 * s, hops + 3 * s, partner, 7, k),
+            )
+        )
+
+    def each(entries, act, k):
         for condition, make in entries:
             if condition is True:
-                act(make())
+                act(make(k))
             else:
 
                 @pl.when(condition)
                 def _(make=make):
-                    act(make())
-
-    def arrived(d):
-        @pl.when(inside(position - d))
+                    act(make(k))
+
+    def arrived(d, k):
+        @pl.when(inside(position - d) & (side != -d))
         def _():
-            query_copy(hops, d + hops, partner, 0).wait_recv()
-
-    def out_copy(slot, target):
+            query_copy(hops, d + hops, partner, 0, k).wait_recv()
+
+    def out_copy(slot, target, head=None):
+        part = slice(0, width)
+        if head is not None:
+            part = slice(head * HEAD_DIM, (head + 1) * HEAD_DIM)
         return pltpu.make_async_remote_copy(
-            src_ref=out_ref.at[slot], dst_ref=back_ref.at[slot], send_sem=o_send.at[slot],
+            src_ref=out_ref.at[slot, part], dst_ref=back_ref.at[slot, part], send_sem=o_send.at[slot],
             recv_sem=o_recv.at[slot], device_id=(target, mine), device_id_type=MESH,
         )
 
@@ -285,51 +307,65 @@
             recv_sem=s_recv.at[slot], device_id=(target, mine), device_id_type=MESH,
         )
 
-    each(sends, lambda copy: copy.start())
+    for k in range(PIECES):
+        each(sends, lambda copy: copy.start(), k)
 
     for d in offsets:
 
         @pl.when(jnp.logical_not(inside(position - d)))
         def _(d=d):
-            pack_ref[d + hops] = jnp.zeros((rows + EXTRA, width), jnp.bfloat16)
-
-    def run(columns, slots):
+            pack_ref[d + hops] = jnp.zeros(pack_ref.shape[1:], jnp.bfloat16)
+
+    def run(columns, slots, after):
         attend(
-            columns, slots, pack_ref, keys_ref, values_ref, slope_ref, score_ref, out_ref, stat_ref
-        )
-
-    def give(d):
-        @pl.when(inside(position - d))
-        def _():
-            stat_copy(d + hops, position - d).start()
-            out_copy(d + hops, position - d).start()
+            columns, slots, after, pack_ref, keys_ref, values_ref, slope_ref, score_ref, out_ref,
+            stat_ref,
+        )
+
+    def forward(k):
+        query_copy(hops, hops - side, partner, 0, k).wait_recv()
+        each(across, lambda copy: copy.start(), k)
+        arrived(2, k)
+        arrived(-2, k)
+        each(onward, lambda copy: copy.start(), k)
+
+    def give(ds):
+        def after(head):
+            for d in ds:
+
+                @pl.when(inside(position - d))
+                def _(d=d):
+                    if head == groups - 1:
+                        stat_copy(d + hops, position - d).start()
+                    out_copy(d + hops, position - d, head).start()
+
+        return after
+
+    def between(head):
+        if head in (1, 3):
+            forward(head // 2)
 
     loads[0].wait()
     prepare_keys(k_ref, keys_ref)
     loads[1].wait()
     prepare_values(v_ref, values_ref)
-    run([(0, 1)], [hops])
-    arrived(2)
-    arrived(-2)
-    each(onward, lambda copy: copy.start())
-    for hop in (2, 1, 4, 3):
-        if hop == 1:
-            arrived(4)
-            arrived(-4)
-            each(final, lambda copy: copy.start())
-        if hop in (1, 3):
-            for d in (hop, -hop):
-                arrived(d)
-        if hop == 4:
-            for d in (hop, -hop):
-
-                @pl.when(inside(position - d))
-                def _(d=d):
-                    run([(abs(d), 1 if d > 0 else -1)], [d + hops])
-        else:
-            run([(hop, 1), (hop, -1)], [hop + hops, hops - hop])
-        for d in (hop, -hop):
-            give(d)
+    run([(0, 1)], [hops], between)
+    run([(2, 1), (2, -1)], [hops + 2, hops - 2], give((2, -2)))
+    for k in range(PIECES):
+        arrived(4, k)
+        arrived(-4, k)
+        each(final, lambda copy: copy.start(), k)
+    for d in (4, -4):
+
+        @pl.when(inside(position - d))
+        def _(d=d):
+            run([(4, d // 4)], [d + hops], give((d,)))
+
+    for hop in (1, 3):
+        for k in range(PIECES):
+            arrived(hop, k)
+            arrived(-hop, k)
+        run([(hop, 1), (hop, -1)], [hop + hops, hops - hop], give((hop, -hop)))
 
     back_stat_ref[hops] = stat_ref[hops]
     for d in offsets:
@@ -393,7 +429,8 @@
         result = result + head_ref[r - 1].astype(jnp.float32)
     result_ref[...] = result
 
-    each(sends + onward + final, lambda copy: copy.wait_send())
+    for k in range(PIECES):
+        each(sends + onward + across + final, lambda copy: copy.wait_send(), k)
     for r in range(1, head_count):
         head_copy(r, lax.rem(mine + r, head_count)).wait_send()
     for d in offsets:
@@ -426,7 +463,7 @@
             pltpu.VMEM((groups, bins, LANES), jnp.bfloat16),
             pltpu.VMEM((width, bins), jnp.bfloat16),
             pltpu.VMEM(w_out.shape, jnp.bfloat16),
-            pltpu.VMEM((slots, rows + EXTRA, width), jnp.bfloat16),
+            pltpu.VMEM((slots, EXTRA + rows * width // LANES, LANES), jnp.bfloat16),
             pltpu.VMEM((slots, width, rows), jnp.bfloat16),
             pltpu.VMEM((slots, 2 * groups, rows), jnp.float32),
             pltpu.VMEM((slots, width, rows), jnp.bfloat16),
@@ -437,7 +474,8 @@
             pltpu.VMEM((head_count - 1, rows, piece), jnp.bfloat16),
             pltpu.SemaphoreType.DMA((3,)),
         ]
-        + [pltpu.SemaphoreType.DMA((slots,))] * 6
+        + [pltpu.SemaphoreType.DMA((slots, PIECES))] * 2
+        + [pltpu.SemaphoreType.DMA((slots,))] * 4
         + [pltpu.SemaphoreType.DMA((head_count - 1,))] * 2,
         compiler_params=pltpu.CompilerParams(collective_id=0, has_side_effects=True),
     )(

time: 37.1 us -> 36.2 us (0.976)
  Pallas kernels: 35.3 us -> 34.4 us
    pallas_call x1, Pallas kernels: 35.3 us -> 34.4 us  [local(): pl.pallas_call(functools.partial(attend_kernel, hops, seq_count, head_cou...]
where the time goes in v2:
time: 36.2 us; the launch traced here: 36 us
  Pallas kernels  34.4 us (95%)
  other arithmetic  1.58 us (4%)
    pallas_call x1, Pallas kernels, local(): pl.pallas_call(functools.partial(attend_kernel, hops, seq_count, head_cou...  34.4 us
    convert_element_type x1, other arithmetic, local(): return result.astype(jnp.bfloat16)  1.58 us

profile of v2, /device:TPU:1, one launch (start us, length us, event | category | flops | bytes accessed | tf_op | source)
XLA Modules:
  0.0 36.0 jit_solution(16245447006782802858)
XLA Ops:
  0.0 34.4 %shard_map.91 = f32[128,384]{1,0:T(8,128)} custom-call(bf16[128,384]{1,0:T(8,128)(2,1)} %query_ref.1, s32[1,128]{1,0:T(1,128)} %bitcast.3, s32[1,128]{1,0:T(1,128)} %bitcast.4, s32[1,128]{1,0:T(1,128)} %bitcast.5, bf16[128,384]{1,0:T(8,128)(2,1)} %embed_ref.1, bf16[2048,384]{1,0:T(8,128)(2,1)} %k_hbm.1, bf16[2048,384]{1,0:T(8,128)(2,1)} %v_hbm.1, ...), custom_call_target="tpu_custom_call" | custom-call | tf_op jit(solution)/shard_map/pallas_call | solution.py:455
  34.4 1.6 %convert_element_type.3 = bf16[128,384]{1,0:T(8,128)(2,1)} convert(f32[128,384]{1,0:T(8,128)} %shard_map.91) | non-fusion elementwise | flops 49152 | bytes 294912 | tf_op jit(solution)/shard_map/convert_element_type | solution.py:492

commit v3 on v2

--- a/solution.py
+++ b/solution.py
@@ -252,24 +252,22 @@
         (inside(position + 2), lambda k: query_copy(hops, hops + 2, position + 2, 1, k)),
         (inside(position - 2), lambda k: query_copy(hops, hops - 2, position - 2, 2, k)),
     ]
-    onward, across, final = [], [], []
+    onward, final = [], []
     for s, send in ((1, 3), (-1, 5)):
-        onward.append(
+        onward += [
             (
                 inside(position - 2 * s) & inside(position + 2 * s),
                 lambda k, s=s, send=send: query_copy(
                     hops + 2 * s, hops + 4 * s, position + 2 * s, send, k
                 ),
-            )
-        )
-        across.append(
+            ),
             (
-                inside(position + 2 * s),
+                inside(position - 2 * s),
                 lambda k, s=s, send=send: query_copy(
-                    hops - side, hops + 2 * s - side, position + 2 * s, send + 1, k
+                    hops + 2 * s, hops + 2 * s + side, partner, send + 1, k
                 ),
-            )
-        )
+            ),
+        ]
         final.append(
             (
                 inside(position - 4 * s) & (side == -s),
@@ -288,7 +286,7 @@
                     act(make(k))
 
     def arrived(d, k):
-        @pl.when(inside(position - d) & (side != -d))
+        @pl.when(inside(position - d))
         def _():
             query_copy(hops, d + hops, partner, 0, k).wait_recv()
 
@@ -323,8 +321,6 @@
         )
 
     def forward(k):
-        query_copy(hops, hops - side, partner, 0, k).wait_recv()
-        each(across, lambda copy: copy.start(), k)
         arrived(2, k)
         arrived(-2, k)
         each(onward, lambda copy: copy.start(), k)
@@ -409,30 +405,65 @@
     pooled = sum_ref[...].T.astype(jnp.bfloat16)
     loads[2].wait()
 
-    def head_copy(r, target):
+    chips = head_count // 2
+    core = lax.rem(mine, 2)
+    twin = mine + 1 - 2 * core
+    half = rows // 2
+
+    def head_copy(n, target):
         return pltpu.make_async_remote_copy(
-            src_ref=part_ref.at[r - 1], dst_ref=head_ref.at[r - 1], send_sem=h_send.at[r - 1],
-            recv_sem=h_recv.at[r - 1], device_id=(position, target), device_id_type=MESH,
-        )
+            src_ref=part_ref.at[n], dst_ref=head_ref.at[n], send_sem=h_send.at[n],
+            recv_sem=h_recv.at[n], device_id=(position, target), device_id_type=MESH,
+        )
+
+    exchanged = []
+
+    def pass_on(n, value, target):
+        part_ref[n] = value.astype(jnp.bfloat16)
+        exchanged.append((n, target))
+        head_copy(n, target).start()
+
+    def taken(n):
+        head_copy(n, twin).wait_recv()
+        return head_ref[n].astype(jnp.float32)
 
     def share(target):
         columns = pl.ds(pl.multiple_of(target * piece, piece), piece)
         return jnp.dot(pooled, w_ref[:, columns], preferred_element_type=jnp.float32)
 
-    for r in range(1, head_count):
-        target = lax.rem(mine + r, head_count)
-        part_ref[r - 1] = share(target).astype(jnp.bfloat16)
-        head_copy(r, target).start()
+    def elsewhere(k, which):
+        return lax.rem(mine - core + 2 * k, head_count) + which
+
+    kept = []
+    for k in range(1, chips):
+        base = 4 * (k - 1)
+        value = share(elsewhere(k, 1 - core))
+        pass_on(base + 2, value[half:], twin)
+        pass_on(base + 1, value[:half], elsewhere(k, 1 - core))
+        value = share(elsewhere(k, core))
+        pass_on(base, value[:half], elsewhere(k, core))
+        kept.append(value[half:])
+    last = 4 * (chips - 1)
+    value = share(twin)
+    pass_on(last, value[:half], twin)
+    pass_on(last + 1, value[half:], twin)
+    for k in range(1, chips):
+        base = 4 * (k - 1)
+        pass_on(base + 3, kept[k - 1] + taken(base + 2), elsewhere(k, core))
     result = share(mine)
-    for r in range(1, head_count):
-        head_copy(r, lax.rem(mine + r, head_count)).wait_recv()
-        result = result + head_ref[r - 1].astype(jnp.float32)
-    result_ref[...] = result
+    upper = result[:half] + taken(last)
+    lower = result[half:] + taken(last + 1)
+    for k in range(1, chips):
+        base = 4 * (k - 1)
+        upper = upper + taken(base) + taken(base + 1)
+        lower = lower + taken(base + 3)
+    result_ref[:half, :] = upper
+    result_ref[half:, :] = lower
 
     for k in range(PIECES):
-        each(sends + onward + across + final, lambda copy: copy.wait_send(), k)
-    for r in range(1, head_count):
-        head_copy(r, lax.rem(mine + r, head_count)).wait_send()
+        each(sends + onward + final, lambda copy: copy.wait_send(), k)
+    for n, target in exchanged:
+        head_copy(n, target).wait_send()
     for d in offsets:
 
         @pl.when(inside(position - d))
@@ -470,13 +501,13 @@
             pltpu.VMEM((slots, 2 * groups, rows), jnp.float32),
             pltpu.VMEM((2, bins, 2 * rows), jnp.float32),
             pltpu.VMEM((width, rows), jnp.float32),
-            pltpu.VMEM((head_count - 1, rows, piece), jnp.bfloat16),
-            pltpu.VMEM((head_count - 1, rows, piece), jnp.bfloat16),
+            pltpu.VMEM((2 * head_count - 2, rows // 2, piece), jnp.bfloat16),
+            pltpu.VMEM((2 * head_count - 2, rows // 2, piece), jnp.bfloat16),
             pltpu.SemaphoreType.DMA((3,)),
         ]
         + [pltpu.SemaphoreType.DMA((slots, PIECES))] * 2
         + [pltpu.SemaphoreType.DMA((slots,))] * 4
-        + [pltpu.SemaphoreType.DMA((head_count - 1,))] * 2,
+        + [pltpu.SemaphoreType.DMA((2 * head_count - 2,))] * 2,
         compiler_params=pltpu.CompilerParams(collective_id=0, has_side_effects=True),
     )(
         queries,

time: 36.2 us -> 35 us (0.967)
  the two profiles are of different devices: /device:TPU:1 before, /device:TPU:2 now
where the time goes in v3:
time: 35 us; the launch traced here: 34.8 us
  Pallas kernels  33.2 us (95%)
  other arithmetic  1.58 us (5%)
    pallas_call x1, Pallas kernels, local(): pl.pallas_call(functools.partial(attend_kernel, hops, seq_count, head_cou...  33.2 us
    convert_element_type x1, other arithmetic, local(): return result.astype(jnp.bfloat16)  1.58 us

profile of v3, /device:TPU:2, one launch (start us, length us, event | category | flops | bytes accessed | tf_op | source)
XLA Modules:
  0.0 34.8 jit_solution(16262709518019631095)
XLA Ops:
  0.0 33.2 %shard_map.91 = f32[128,384]{1,0:T(8,128)} custom-call(bf16[128,384]{1,0:T(8,128)(2,1)} %query_ref.1, s32[1,128]{1,0:T(1,128)} %bitcast.3, s32[1,128]{1,0:T(1,128)} %bitcast.4, s32[1,128]{1,0:T(1,128)} %bitcast.5, bf16[128,384]{1,0:T(8,128)(2,1)} %embed_ref.1, bf16[2048,384]{1,0:T(8,128)(2,1)} %k_hbm.1, bf16[2048,384]{1,0:T(8,128)(2,1)} %v_hbm.1, ...), custom_call_target="tpu_custom_call" | custom-call | tf_op jit(solution)/shard_map/pallas_call | solution.py:486
  33.2 1.6 %convert_element_type.3 = bf16[128,384]{1,0:T(8,128)(2,1)} convert(f32[128,384]{1,0:T(8,128)} %shard_map.91) | non-fusion elementwise | flops 49152 | bytes 294912 | tf_op jit(solution)/shard_map/convert_element_type | solution.py:523
